TPU v7x, 32 devices: a whole 2x2x4 slice. The times are simulated.
32 devices in a mesh: groups: 2 (over y), blk: 4 (over z), head: 4 (over x, core).
Axes of the slice: x: 2, y: 2, z: 4, core: 2. Of those that a mesh axis runs over, the one named last changes fastest.
Arguments:
- ctx_query: bfloat16 [4096, 8192], P(('groups', 'blk'), 'head'), parts along dimension 0, may hold values from -5 to 5
- ctx_key: bfloat16 [4096, 1024], P(('groups', 'blk'), 'head'), parts along dimension 0, may hold values from -5 to 5
- ctx_value: bfloat16 [4096, 1024], P(('groups', 'blk'), 'head'), parts along dimension 0, may hold values from -4.5 to 4.5
- opt_query: bfloat16 [128, 8192], P(('groups', 'blk'), 'head'), parts along dimension 0, may hold values from -5 to 5
- opt_owner: int32 [128], P('groups'), parts along dimension 0, may hold values from 0 to 3, as said below
- opt_slot: int32 [128], P('groups'), parts along dimension 0, may hold values from 0 to 31, as said below
- opt_length: int32 [128], P('groups'), parts along dimension 0, may hold values from 512 to 2048
Outputs:
- ctx_out: bfloat16 [4096, 8192], P(('groups', 'blk'), 'head'), parts along dimension 0
- opt_out: bfloat16 [256, 8192], P(('groups', 'blk'), 'head'), parts along dimension 0
There are 2 independent parts, one for each index of `groups`. A program takes and returns all parts, laid end to end along the dimension named above; each array names one. Nothing has to cross between parts.
Inputs may be any that keep to these rules, and one draw needn't show every extreme that they name: `opt_owner`: each option token has its own pair of owner block and slot; no block owns more than 32 option tokens, and one block owns exactly 32. `opt_slot`: slots of one owner are distinct.
All inputs are finite; a program needn't handle non-finite values.
Results may differ from a plain program's by a relative error of at most 0.017.
Values may be sent and summed in bfloat16 or wider, within the bound.
A program may use at most 64 MiB of HBM per device.

v0:
```python
import jax
import jax.numpy as jnp
from jax import lax
from jax.sharding import PartitionSpec as P

HD = 128
HQ = 64
KVH = 8
CAP = 32


def from_root(value, axis, root):
    mine = lax.axis_index(axis) == root
    return lax.psum(jnp.where(mine, value, jnp.zeros_like(value)), axis)


def soft_parts(query_head, keys, values, masks, scale):
    scores = []
    for key_part, mask_part in zip(keys, masks):
        raw = (
            jnp.einsum("td,sd->ts", query_head, key_part, preferred_element_type=jnp.float32)
            * scale
        )
        scores.append(jnp.where(mask_part, raw, -1e30))
    top = jnp.max(scores[0], axis=1)
    for extra in scores[1:]:
        top = jnp.maximum(top, jnp.max(extra, axis=1))
    total = jnp.zeros_like(top)
    accum = jnp.zeros((query_head.shape[0], values[0].shape[1]), jnp.float32)
    for score_part, value_part in zip(scores, values):
        expo = jnp.exp(score_part - top[:, None])
        total = total + jnp.sum(expo, axis=1)
        accum = accum + jnp.dot(
            expo.astype(jnp.bfloat16), value_part, preferred_element_type=jnp.float32
        )
    return (accum / total[:, None], top, total)


def body(ctx_query, ctx_key, ctx_value, opt_query, opt_owner, opt_slot, opt_length):
    group_size = HQ // KVH
    scale = HD ** (-0.5)
    block_index = lax.axis_index("blk")
    block_count = lax.axis_size("blk")
    rows = ctx_query.shape[0]
    local_heads = ctx_query.shape[1] // HD
    anchor_key, anchor_value = (from_root(ctx_key, "blk", 0), from_root(ctx_value, "blk", 0))
    spots = jnp.arange(rows, dtype=jnp.int32)
    causal = spots[:, None] >= spots[None, :]
    anchor_mask = jnp.broadcast_to(block_index > 0, (rows, rows))

    def phase_one(head_id, result):
        group = head_id // group_size
        query_head = lax.dynamic_slice_in_dim(ctx_query, head_id * HD, HD, 1)
        key_local = lax.dynamic_slice_in_dim(ctx_key, group * HD, HD, 1)
        value_local = lax.dynamic_slice_in_dim(ctx_value, group * HD, HD, 1)
        key_anchor = lax.dynamic_slice_in_dim(anchor_key, group * HD, HD, 1)
        value_anchor = lax.dynamic_slice_in_dim(anchor_value, group * HD, HD, 1)
        output, top, total = soft_parts(
            query_head,
            (key_anchor, key_local),
            (value_anchor, value_local),
            (anchor_mask, causal),
            scale,
        )
        return lax.dynamic_update_slice_in_dim(result, output.astype(jnp.bfloat16), head_id * HD, 1)

    ctx_out = lax.fori_loop(0, local_heads, phase_one, jnp.zeros(ctx_query.shape, jnp.bfloat16))
    all_queries = lax.all_gather(opt_query, "blk", axis=0, tiled=True)
    options = all_queries.shape[0]
    count = jnp.clip(opt_length - block_index * rows, 0, rows)
    live = count > 0
    visible = spots[None, :] < count[:, None]

    def phase_two(head_id, carry):
        partial_value, stats = carry
        group = head_id // group_size
        query_head = lax.dynamic_slice_in_dim(all_queries, head_id * HD, HD, 1)
        key_local = lax.dynamic_slice_in_dim(ctx_key, group * HD, HD, 1)
        value_local = lax.dynamic_slice_in_dim(ctx_value, group * HD, HD, 1)
        output, top, total = soft_parts(query_head, (key_local,), (value_local,), (visible,), scale)
        output = jnp.where(live[:, None], output, 0.0).astype(jnp.bfloat16)
        stat = jnp.where(live, top + jnp.log(total), -1e30)
        partial_value = lax.dynamic_update_slice_in_dim(partial_value, output, head_id * HD, 1)
        stats = lax.dynamic_update_slice_in_dim(stats, stat[:, None], head_id, 1)
        return (partial_value, stats)

    start = (
        jnp.zeros((options, local_heads * HD), jnp.bfloat16),
        jnp.zeros((options, local_heads), jnp.float32),
    )
    partial_value, stats = lax.fori_loop(0, local_heads, phase_two, start)
    slot_total = CAP * block_count
    where_to = opt_owner * CAP + opt_slot
    top_all = lax.pmax(stats, "blk")
    weight = jnp.exp(stats - top_all)
    weight_sum = lax.psum(weight, "blk")
    share = weight / weight_sum
    term = (
        partial_value.reshape(options, local_heads, HD).astype(jnp.float32) * share[:, :, None]
    ).reshape(options, local_heads * HD)
    buffer = jnp.zeros((slot_total, local_heads * HD), jnp.float32).at[where_to].set(term)
    opt_out = lax.psum_scatter(buffer.astype(jnp.bfloat16), "blk", scatter_dimension=0, tiled=True)
    return (ctx_out, opt_out)


def solution(mesh):
    return jax.shard_map(
        body,
        mesh=mesh,
        in_specs=(
            P(("groups", "blk"), "head"),
            P(("groups", "blk"), "head"),
            P(("groups", "blk"), "head"),
            P(("groups", "blk"), "head"),
            P("groups"),
            P("groups"),
            P("groups"),
        ),
        out_specs=(P(("groups", "blk"), "head"), P(("groups", "blk"), "head")),
        check_vma=False,
    )
```

profile of v0, /device:TPU:0, one launch (start us, length us, event | category | flops | bytes accessed | tf_op | source)
XLA Modules:
  0.0 127.9 jit_solution(5371850114910661687)
XLA Ops:
  7.2 1.9 %broadcast_select_fusion = (bf16[512,256]{1,0:T(8,128)(2,1)}, bf16[512,256]{1,0:T(8,128)(2,1)}) fusion(bf16[512,256]{1,0:T(8,128)(2,1)} %param.13, pred[]{:T(512)S(6)} %eq.4, bf16[512,256]{1,0:T(8,128)(2,1)} %param.12), kind=kLoop, calls=%fused_computation.54 | loop fusion | flops 262144 | bytes 1048577 | tf_op jit(solution)/shard_map/jit(_where)/select_n | solution.py:14
  9.2 15.8 %all_gather.3 = bf16[64,2048]{1,0:T(8,128)(2,1)S(1)} all-gather(bf16[16,2048]{1,0:T(8,128)(2,1)} %param.14), channel_id=1, replica_groups=mesh['groups'=2,'blk'=4,'head'=4] {'blk'}, dimensions={0}, use_global_device_ids=true | all-gather | bytes 327680 | tf_op jit(solution)/shard_map/all_gather | solution.py:68
  25.0 0.7 broadcast_compare_fusion
  25.7 12.9 %while.35 = (s32[]{:T(128)}, bf16[64,2048]{1,0:T(8,128)(2,1)S(1)}, f32[64,16]{0,1:T(8,128)S(1)}, pred[64]{0:T(512)(128)(4,1)S(1)}, bf16[64,2048]{1,0:T(8,128)(2,...) while((s32[]{:T(128)}, bf16[64,2048]{1,0:T(8,128)(2,1)S(1)}, ...), condition=%wide.region_11.12_spmd.clone, body=%wide.region_8.11_spmd.clone.sunk | while | flops 17063952 | bytes 692635 | solution.py:91
  38.6 11.7 %pmax.7 = f32[64,16]{0,1:T(8,128)S(1)} all-reduce(f32[64,16]{0,1:T(8,128)S(1)} %get-tuple-element.425), channel_id=1, replica_groups=mesh['groups'=2,'blk'=4,'head'=4] {'blk'}, use_global_device_ids=true, to_apply=%region_12.13 | all-reduce | flops 1024 | bytes 8192 | tf_op jit(solution)/shard_map/pmax | solution.py:94
  50.4 8.5 %psum.23 = f32[64,16]{0,1:T(8,128)S(1)} all-reduce(f32[64,16]{0,1:T(8,128)S(1)} %subtract_exponential_fusion.3), channel_id=1, replica_groups=mesh['groups'=2,'blk'=4,'head'=4] {'blk'}, use_global_device_ids=true, to_apply=%region_13.14 | all-reduce | flops 1024 | bytes 8192 | tf_op jit(solution)/shard_map/psum | solution.py:96
  59.2 1.3 %scatter_custom_fusion = f32[128,2048]{1,0:T(8,128)S(1)} fusion(s32[64]{0:T(128)S(1)} %compare_select_fusion, f32[8,8,16,128]{3,2,1,0:T(8,128)S(1)} %bitcast.8, bf16[64,2048]{1,0:T(8,128)(2,1)S(1)} %get-tuple-element.424, f32[]{:T(128)} %constant.275.clone.1), kind=kCustom, calls=%fused_computation.50 | custom fusion | flops 262144 | bytes 1835012 | tf_op jit(solution)/shard_map/scatter | solution.py:101
  60.6 0.9 convert_element_type.58
  61.8 0.6 copy-done.5
  62.5 57.1 %while.34 = (s32[]{:T(128)}, bf16[512,2048]{1,0:T(8,128)(2,1)S(1)}, bf16[512,2048]{1,0:T(8,128)(2,1)}, bf16[512,256]{1,0:T(8,128)(2,1)S(1)}, bf16[512,256]{1,0:T...) while((s32[]{:T(128)}, bf16[512,2048]{1,0:T(8,128)(2,1)S(1)}, ...), condition=%wide.region_7.8_spmd.clone, body=%wide.region_2.7_spmd.clone.sunk | while | flops 272563200 | bytes 7762787 | solution.py:67
  62.5 1.2 fusion.68
  63.8 1.2 fusion.69
  66.1 1.2 fusion.68
  67.3 1.2 fusion.69
  69.7 1.2 fusion.68
  70.9 1.2 fusion.69
  72.8 0.4 fusion.72
  73.3 1.2 fusion.68
  74.5 1.2 fusion.69
  76.8 1.2 fusion.68
  78.1 1.2 fusion.69
  80.0 0.4 fusion.72
  80.4 1.2 fusion.68
  81.6 1.2 fusion.69
  83.5 0.4 fusion.72
  84.0 1.2 fusion.68
  85.2 1.2 fusion.69
  87.1 0.4 fusion.72
  87.6 1.2 fusion.68
  88.8 1.2 fusion.69
  90.7 0.4 fusion.72
  91.1 1.2 fusion.68
  92.4 1.2 fusion.69
  94.7 1.2 fusion.68
  95.9 1.2 fusion.69
  98.3 1.2 fusion.68
  99.5 1.2 fusion.69
  101.9 1.2 fusion.68
  103.1 1.2 fusion.69
  105.4 1.2 fusion.68
  106.7 1.2 fusion.69
  109.0 1.2 fusion.68
  110.2 1.2 fusion.69
  112.6 1.2 fusion.68
  113.8 1.2 fusion.69
  116.2 1.2 fusion.68
  117.4 1.2 fusion.69
  119.7 1.3 %copy-done.1 = bf16[512,2048]{1,0:T(8,128)(2,1)} copy-done((bf16[512,2048]{1,0:T(8,128)(2,1)}, bf16[512,2048]{1,0:T(8,128)(2,1)S(1)}, u32[]{:S(2)}) %copy-start.1) | copy-done | bytes 2097176
  (183 shorter events, 28.1 us)
Async XLA Ops:
  7.2 18.5 %copy-start.4 = (bf16[512,256]{1,0:T(8,128)(2,1)S(1)}, bf16[512,256]{1,0:T(8,128)(2,1)}, u32[]{:S(2)}) copy-start(bf16[512,256]{1,0:T(8,128)(2,1)} %param.13) | copy-start | bytes 786436
  7.2 18.5 %copy-start = (bf16[512,256]{1,0:T(8,128)(2,1)S(1)}, bf16[512,256]{1,0:T(8,128)(2,1)}, u32[]{:S(2)}) copy-start(bf16[512,256]{1,0:T(8,128)(2,1)} %param.12) | copy-start | bytes 786436
  7.2 54.3 %all-reduce.3.cloned.1.call-start = ((), (), s32[]{:S(2)}) async-start(), calls=%async_computation.2 | async-start | bytes 1048576 | tf_op jit(solution)/shard_map/psum | solution.py:14
  9.2 110.5 %reduce-scatter.2.cloned.1.call-start = ((), (), s32[]{:S(2)}) async-start(), calls=%async_computation.1 | async-start | bytes 655360 | tf_op jit(solution)/shard_map/reduce_scatter | solution.py:102
  25.7 33.3 %copy-start.6 = (s32[64]{0:T(128)S(1)}, s32[64]{0:T(128)}, u32[]{:S(2)}) copy-start(s32[64]{0:T(128)} %param.16) | copy-start | bytes 772
  25.7 33.3 %copy-start.7 = (s32[64]{0:T(128)S(1)}, s32[64]{0:T(128)}, u32[]{:S(2)}) copy-start(s32[64]{0:T(128)} %param.15) | copy-start | bytes 772
  61.4 0.9 copy-start.5
  61.5 1.0 copy-start.2
  61.5 1.1 copy-start.3
  119.7 1.3 %copy-start.1 = (bf16[512,2048]{1,0:T(8,128)(2,1)}, bf16[512,2048]{1,0:T(8,128)(2,1)S(1)}, u32[]{:S(2)}) copy-start(bf16[512,2048]{1,0:T(8,128)(2,1)S(1)} %get-tuple-element.421) | copy-start | bytes 6291460
Sparse Core Ops, SparseCore 0:
  11.0 43.1 all-reduce.2
  61.6 21.6 reduce-scatter.1
where the time goes:
time: 129 us; the launch traced here: 128 us
  matrix products  59.5 us (46%)
  blocking collectives  36 us (28%)
  between operations  14.2 us (11%)
  other arithmetic  13 us (10%)
  local copies, waits for them, and re-layouts  3.26 us (3%)
  loops' own time  1.7 us (1%)
    dot_general x48, matrix products, soft_parts(): jnp.einsum('td,sd->ts', query_head, key_part, preferred_element_type=jnp....  43.5 us
    dot_general x48, matrix products, soft_parts(): jnp.dot(expo.astype(jnp.bfloat16), value_part, preferred_element_type=jnp...  15.9 us
    all_gather x1, blocking collectives, body(): all_queries = lax.all_gather(opt_query, 'blk', axis=0, tiled=True)  15.8 us
    pmax x1, blocking collectives, body(): top_all = lax.pmax(stats, 'blk')  11.7 us
    psum x1, blocking collectives, body(): weight_sum = lax.psum(weight, 'blk')  8.52 us
    reduce_sum x32, other arithmetic, soft_parts(): total = total + jnp.sum(expo, axis=1)  7.92 us
  transfers between devices with their start and end apart: 2, of which 0 were waited for; matrix products, arithmetic and copies ran while one was open for 56% of the time, Pallas kernels for 0%

commit v1 on v0

--- a/solution.py
+++ b/solution.py
@@ -93,7 +93,11 @@
     where_to = opt_owner * CAP + opt_slot
     top_all = lax.pmax(stats, "blk")
     weight = jnp.exp(stats - top_all)
-    weight_sum = lax.psum(weight, "blk")
+    weight_sum = weight
+    for hop in (1, 2):
+        weight_sum = weight_sum + lax.ppermute(
+            weight_sum, "blk", [(dev, dev ^ hop) for dev in range(4)]
+        )
     share = weight / weight_sum
     term = (
         partial_value.reshape(options, local_heads, HD).astype(jnp.float32) * share[:, :, None]

time: 129 us -> 129 us (level)
  blocking collectives: 36 us -> 27.8 us
  waiting for transfers between devices: 0.07 us -> 8.22 us
    psum x1 -> x0, blocking collectives: 8.52 us -> none  [body(): weight_sum = lax.psum(weight, 'blk')]
    ppermute x0 -> x2, waiting for transfers between devices: none -> 8.15 us  [body(): lax.ppermute(weight_sum, 'blk', [(dev, dev ^ hop) for dev in range(4)])]
  transfers between devices with their start and end apart: 2 -> 4, of which waited for: 0 -> 2; matrix products, arithmetic and copies ran while one was open for 56% -> 56% of each run, Pallas kernels for 0% -> 0%
where the time goes in v1:
time: 129 us; the launch traced here: 128 us
  matrix products  59.5 us (46%)
  blocking collectives  27.8 us (22%)
  between operations  14.2 us (11%)
  other arithmetic  13 us (10%)
  waiting for transfers between devices  8.22 us (6%)
  local copies, waits for them, and re-layouts  3.26 us (3%)
  loops' own time  1.71 us (1%)
    dot_general x48, matrix products, soft_parts(): jnp.einsum('td,sd->ts', query_head, key_part, preferred_element_type=jnp....  43.6 us
    dot_general x48, matrix products, soft_parts(): jnp.dot(expo.astype(jnp.bfloat16), value_part, preferred_element_type=jnp...  15.9 us
    all_gather x1, blocking collectives, body(): all_queries = lax.all_gather(opt_query, 'blk', axis=0, tiled=True)  15.8 us
    pmax x1, blocking collectives, body(): top_all = lax.pmax(stats, 'blk')  12 us
    ppermute x2, waiting for transfers between devices, body(): lax.ppermute(weight_sum, 'blk', [(dev, dev ^ hop) for dev in range(4)])  8.15 us
    reduce_sum x32, other arithmetic, soft_parts(): total = total + jnp.sum(expo, axis=1)  7.92 us
  transfers between devices with their start and end apart: 4, of which 2 were waited for; matrix products, arithmetic and copies ran while one was open for 56% of the time, Pallas kernels for 0%

profile of v1, /device:TPU:0, one launch (start us, length us, event | category | flops | bytes accessed | tf_op | source)
XLA Modules:
  0.0 127.9 jit_solution(10184053113526831672)
XLA Ops:
  7.2 1.9 %broadcast_select_fusion = (bf16[512,256]{1,0:T(8,128)(2,1)}, bf16[512,256]{1,0:T(8,128)(2,1)}) fusion(bf16[512,256]{1,0:T(8,128)(2,1)} %param.13, pred[]{:T(512)S(6)} %eq.4, bf16[512,256]{1,0:T(8,128)(2,1)} %param.12), kind=kLoop, calls=%fused_computation.54 | loop fusion | flops 262144 | bytes 1048577 | tf_op jit(solution)/shard_map/jit(_where)/select_n | solution.py:14
  9.2 15.8 %all_gather.3 = bf16[64,2048]{1,0:T(8,128)(2,1)S(1)} all-gather(bf16[16,2048]{1,0:T(8,128)(2,1)} %param.14), channel_id=1, replica_groups=mesh['groups'=2,'blk'=4,'head'=4] {'blk'}, dimensions={0}, use_global_device_ids=true | all-gather | bytes 327680 | tf_op jit(solution)/shard_map/all_gather | solution.py:68
  25.0 0.7 broadcast_compare_fusion
  25.7 12.9 %while.35 = (s32[]{:T(128)}, bf16[64,2048]{1,0:T(8,128)(2,1)S(1)}, f32[64,16]{0,1:T(8,128)S(1)}, pred[64]{0:T(512)(128)(4,1)S(1)}, bf16[64,2048]{1,0:T(8,128)(2,...) while((s32[]{:T(128)}, bf16[64,2048]{1,0:T(8,128)(2,1)S(1)}, ...), condition=%wide.region_11.12_spmd.clone, body=%wide.region_8.11_spmd.clone.sunk | while | flops 17063952 | bytes 692635 | solution.py:91
  38.6 12.0 %pmax.7 = f32[64,16]{0,1:T(8,128)S(1)} all-reduce(f32[64,16]{0,1:T(8,128)S(1)} %get-tuple-element.425), channel_id=1, replica_groups=mesh['groups'=2,'blk'=4,'head'=4] {'blk'}, use_global_device_ids=true, to_apply=%region_12.13 | all-reduce | flops 1024 | bytes 8192 | tf_op jit(solution)/shard_map/pmax | solution.py:94
  50.8 3.6 %collective-permute-done = f32[64,16]{0,1:T(8,128)S(1)} collective-permute-done((f32[64,16]{0,1:T(8,128)S(1)}, f32[64,16]{0,1:T(8,128)S(1)}, u32[]{:S(2)}, u32[]{:S(2)}) %collective-permute-start) | collective-permute-done | bytes 4128 | tf_op jit(solution)/shard_map/ppermute | solution.py:98
  54.4 4.5 %collective-permute-done.1 = f32[64,16]{0,1:T(8,128)S(1)} collective-permute-done((f32[64,16]{0,1:T(8,128)S(1)}, f32[64,16]{0,1:T(8,128)S(1)}, u32[]{:S(2)}, u32[]{:S(2)}) %collective-permute-start.1) | collective-permute-done | bytes 4128 | tf_op jit(solution)/shard_map/ppermute | solution.py:98
  59.2 1.3 %scatter_custom_fusion = f32[128,2048]{1,0:T(8,128)S(1)} fusion(s32[64]{0:T(128)S(1)} %compare_select_fusion, f32[8,8,16,128]{3,2,1,0:T(8,128)S(1)} %bitcast.8, bf16[64,2048]{1,0:T(8,128)(2,1)S(1)} %get-tuple-element.424, f32[]{:T(128)} %constant.275.clone.1), kind=kCustom, calls=%fused_computation.50 | custom fusion | flops 262144 | bytes 1835012 | tf_op jit(solution)/shard_map/scatter | solution.py:105
  60.6 0.9 convert_element_type.58
  61.8 0.6 copy-done.5
  62.6 57.1 %while.34 = (s32[]{:T(128)}, bf16[512,2048]{1,0:T(8,128)(2,1)S(1)}, bf16[512,2048]{1,0:T(8,128)(2,1)}, bf16[512,256]{1,0:T(8,128)(2,1)S(1)}, bf16[512,256]{1,0:T...) while((s32[]{:T(128)}, bf16[512,2048]{1,0:T(8,128)(2,1)S(1)}, ...), condition=%wide.region_7.8_spmd.clone, body=%wide.region_2.7_spmd.clone.sunk | while | flops 272563200 | bytes 7762787 | solution.py:67
  62.6 1.2 fusion.68
  63.8 1.2 fusion.69
  66.1 1.2 fusion.68
  67.4 1.2 fusion.69
  69.3 0.4 fusion.72
  69.7 1.2 fusion.68
  70.9 1.2 fusion.69
  72.8 0.4 fusion.72
  73.3 1.2 fusion.68
  74.5 1.2 fusion.69
  76.9 1.2 fusion.68
  78.1 1.2 fusion.69
  80.0 0.4 fusion.72
  80.4 1.2 fusion.68
  81.7 1.2 fusion.69
  84.0 1.2 fusion.68
  85.2 1.2 fusion.69
  87.6 1.2 fusion.68
  88.8 1.2 fusion.69
  90.7 0.4 fusion.72
  91.2 1.2 fusion.68
  92.4 1.2 fusion.69
  94.7 1.2 fusion.68
  96.0 1.2 fusion.69
  98.3 1.2 fusion.68
  99.5 1.2 fusion.69
  101.9 1.2 fusion.68
  103.1 1.2 fusion.69
  105.5 1.2 fusion.68
  106.7 1.2 fusion.69
  109.0 1.2 fusion.68
  110.2 1.2 fusion.69
  112.6 1.2 fusion.68
  113.8 1.2 fusion.69
  116.2 1.2 fusion.68
  117.4 1.2 fusion.69
  119.8 1.3 %copy-done.1 = bf16[512,2048]{1,0:T(8,128)(2,1)} copy-done((bf16[512,2048]{1,0:T(8,128)(2,1)}, bf16[512,2048]{1,0:T(8,128)(2,1)S(1)}, u32[]{:S(2)}) %copy-start.1) | copy-done | bytes 2097176
  (187 shorter events, 28.6 us)
Async XLA Ops:
  7.2 18.5 %copy-start.4 = (bf16[512,256]{1,0:T(8,128)(2,1)S(1)}, bf16[512,256]{1,0:T(8,128)(2,1)}, u32[]{:S(2)}) copy-start(bf16[512,256]{1,0:T(8,128)(2,1)} %param.13) | copy-start | bytes 786436
  7.2 18.5 %copy-start = (bf16[512,256]{1,0:T(8,128)(2,1)S(1)}, bf16[512,256]{1,0:T(8,128)(2,1)}, u32[]{:S(2)}) copy-start(bf16[512,256]{1,0:T(8,128)(2,1)} %param.12) | copy-start | bytes 786436
  7.2 54.3 %all-reduce.3.cloned.1.call-start = ((), (), s32[]{:S(2)}) async-start(), calls=%async_computation.2 | async-start | bytes 1048576 | tf_op jit(solution)/shard_map/psum | solution.py:14
  9.2 110.6 %reduce-scatter.2.cloned.1.call-start = ((), (), s32[]{:S(2)}) async-start(), calls=%async_computation.1 | async-start | bytes 655360 | tf_op jit(solution)/shard_map/reduce_scatter | solution.py:106
  25.7 28.7 %copy-start.6 = (s32[64]{0:T(128)S(1)}, s32[64]{0:T(128)}, u32[]{:S(2)}) copy-start(s32[64]{0:T(128)} %param.16) | copy-start | bytes 772
  25.7 28.7 %copy-start.7 = (s32[64]{0:T(128)S(1)}, s32[64]{0:T(128)}, u32[]{:S(2)}) copy-start(s32[64]{0:T(128)} %param.15) | copy-start | bytes 772
  50.7 3.7 %collective-permute-start = (f32[64,16]{0,1:T(8,128)S(1)}, f32[64,16]{0,1:T(8,128)S(1)}, u32[]{:S(2)}, u32[]{:S(2)}) collective-permute-start(f32[64,16]{0,1:T(8,128)S(1)} %subtract_exponential_fusion.3), channel_id=1, source_target_pairs={{0,4},{4,0},{8,12},{12,8},{1,5},{5,1},{9,13},{13,9},{2,6},{6,2},{1... | collective-permute-start | bytes 12296 | tf_op jit(solution)/shard_map/ppermute | solution.py:98
  54.4 4.5 %collective-permute-start.1 = (f32[64,16]{0,1:T(8,128)S(1)}, f32[64,16]{0,1:T(8,128)S(1)}, u32[]{:S(2)}, u32[]{:S(2)}) collective-permute-start(f32[64,16]{0,1:T(8,128)S(1)} %add.172), channel_id=1, source_target_pairs={{0,8},{4,12},{8,0},{12,4},{1,9},{5,13},{9,1},{13,5},{2,10},{6,14},... | collective-permute-start | bytes 12296 | tf_op jit(solution)/shard_map/ppermute | solution.py:98
  61.4 0.9 copy-start.5
  61.5 1.0 copy-start.2
  61.5 1.1 copy-start.3
  119.7 1.3 %copy-start.1 = (bf16[512,2048]{1,0:T(8,128)(2,1)}, bf16[512,2048]{1,0:T(8,128)(2,1)S(1)}, u32[]{:S(2)}) copy-start(bf16[512,2048]{1,0:T(8,128)(2,1)S(1)} %get-tuple-element.421) | copy-start | bytes 6291460
Sparse Core Ops, SparseCore 0:
  11.0 42.9 all-reduce.2
  61.6 19.8 reduce-scatter.1
